TPU v7x, 32 devices: a whole 2x2x4 slice. The times are simulated.
32 devices in a mesh: head: 4 (over y, x), batch: 8 (over z, core).
Axes of the slice: x: 2, y: 2, z: 4, core: 2. Of those that a mesh axis runs over, the one named last changes fastest.
Arguments:
- hidden_in: bfloat16 [8, 256, 4096], P('batch', None, 'head')
- w_query: bfloat16 [4096, 4096], P('batch', 'head'), may hold values from -0.09375 to 0.09375
- w_key: bfloat16 [4096, 4096], P('batch', 'head'), may hold values from -0.09375 to 0.09375
- w_value: bfloat16 [4096, 4096], P('batch', 'head'), may hold values from -0.09375 to 0.09375
- w_beta: bfloat16 [4096, 32], P('batch', 'head'), may hold values from -0.09375 to 0.09375
- w_out: bfloat16 [4096, 4096], P('head', 'batch'), may hold values from -0.125 to 0.125
- mem_pos: int32 [8, 2, 64], P('batch'), may hold values from 0 to 127, as said below
- memory_in: float32 [8, 32, 128, 128], P('batch', 'head'), may hold values from -6 to 6
Outputs:
- hidden_out: bfloat16 [8, 256, 4096], P('batch', None, 'head')
- memory_out: float32 [8, 32, 128, 128], P('batch', 'head')
Inputs may be any that keep to these rules, and one draw needn't show every extreme that they name: `mem_pos`: within each sequence and segment the 64 positions are distinct and ascending.
All inputs are finite; a program needn't handle non-finite values.
Results may differ from a plain program's by a relative error of at most 0.005.
Values may be sent and summed in bfloat16 or wider, within the bound.
No kernel may reach another device: no remote copies, remote signals or barrier semaphores. Data moves between devices by JAX's collectives and lax.ppermute only.
A program may use at most 128 MiB of HBM per device.

v0:
```python
import jax
import jax.numpy as jnp
from jax import lax
from jax.sharding import PartitionSpec as P

SEGS = 2
epsilon = 1e-05


def recur(query, keys, values, beta, state):
    highest = lax.Precision.HIGHEST
    readouts = []
    for segment in range(query.shape[1]):
        readouts.append(
            jnp.einsum("bhij,blhj->blhi", state, query[:, segment], precision=highest).astype(
                jnp.bfloat16
            )
        )
        recalled = jnp.einsum("bhij,bmhj->bmhi", state, keys[:, segment], precision=highest)
        change = beta[:, segment][..., None] * (values[:, segment] - recalled)
        state = state + jnp.einsum("bmhi,bmhj->bhij", change, keys[:, segment], precision=highest)
    return (jnp.stack(readouts, axis=1), state)


def body(hidden_in, w_query, w_key, w_value, w_beta, w_out, mem_pos, memory_in):
    seq_count, row_count, local_width = hidden_in.shape
    seg_rows = row_count // SEGS
    mem_count = mem_pos.shape[2]
    local_heads = w_beta.shape[1]
    local_features = w_query.shape[1]
    head_size = local_features // local_heads
    x_float = hidden_in.astype(jnp.float32)
    whole = lax.all_gather(hidden_in, "head", axis=2, tiled=True)
    whole_float = whole.astype(jnp.float32)
    mean_square = jnp.mean(whole_float * whole_float, axis=2, keepdims=True)
    normed = (whole_float * lax.rsqrt(mean_square + epsilon)).astype(jnp.bfloat16)
    full_width = normed.shape[2]
    offsets = (jnp.arange(SEGS, dtype=jnp.int32) * seg_rows)[None, :, None]
    picked = (mem_pos + offsets).reshape(seq_count, SEGS * mem_count)
    memory_rows = jax.vmap(lambda block, where: jnp.take(block, where, axis=0))(normed, picked)
    memory_rows = memory_rows.reshape(seq_count * SEGS * mem_count, full_width)
    token_rows = normed.reshape(seq_count * row_count, full_width)
    piece_query = lax.all_gather(w_query, "batch", axis=0, tiled=True)
    piece_key = lax.all_gather(w_key, "batch", axis=0, tiled=True)
    piece_value = lax.all_gather(w_value, "batch", axis=0, tiled=True)
    piece_beta = lax.all_gather(w_beta, "batch", axis=0, tiled=True)
    query = jnp.dot(token_rows, piece_query, preferred_element_type=jnp.float32)
    keys = jnp.dot(memory_rows, piece_key, preferred_element_type=jnp.float32)
    values = jnp.dot(memory_rows, piece_value, preferred_element_type=jnp.float32)
    logits = jnp.dot(memory_rows, piece_beta, preferred_element_type=jnp.float32)
    query = (query * head_size ** (-0.5)).reshape(seq_count, SEGS, seg_rows, local_heads, head_size)
    keys = keys.reshape(seq_count, SEGS, mem_count, local_heads, head_size)
    keys = keys * lax.rsqrt(jnp.sum(keys * keys, axis=-1, keepdims=True) + 1e-06)
    values = values.reshape(seq_count, SEGS, mem_count, local_heads, head_size)
    beta = jax.nn.sigmoid(logits).reshape(seq_count, SEGS, mem_count, local_heads)
    readout, state = recur(query, keys, values, beta, memory_in)
    readout = readout.reshape(seq_count * row_count, local_features)
    terms = jnp.dot(
        readout,
        lax.all_gather(w_out, "batch", axis=1, tiled=True),
        preferred_element_type=jnp.float32,
    )
    mixed = lax.psum_scatter(terms, "head", scatter_dimension=1, tiled=True)
    hidden_out = (mixed + x_float.reshape(seq_count * row_count, local_width)).astype(jnp.bfloat16)
    return (hidden_out.reshape(hidden_in.shape), state)


def solution(mesh):
    in_specs = (
        P("batch", None, "head"),
        P("batch", "head"),
        P("batch", "head"),
        P("batch", "head"),
        P("batch", "head"),
        P("head", "batch"),
        P("batch", None, None),
        P("batch", "head", None, None),
    )
    out_specs = (P("batch", None, "head"), P("batch", "head", None, None))
    return jax.shard_map(body, mesh=mesh, in_specs=in_specs, out_specs=out_specs, check_vma=False)
```

profile of v0, /device:TPU:0, one launch (start us, length us, event | category | flops | bytes accessed | tf_op | source)
XLA Modules:
  0.0 445.6 jit_solution(10736198151364103323)
XLA Ops:
  10.6 0.8 broadcast_add_fusion
  11.5 15.9 %all_gather.20 = bf16[4096,8]{0,1:T(8,128)(2,1)S(1)} all-gather(bf16[512,8]{0,1:T(8,128)(2,1)} %param.12), channel_id=1, replica_groups=mesh['head'=4,'batch'=8] {'batch'}, dimensions={0}, use_global_device_ids=true | all-gather | bytes 73728 | tf_op jit(solution)/shard_map/all_gather | solution.py:46
  27.4 20.3 %all-gather.6.cloned.1.call-done = bf16[1,256,4096]{2,1,0:T(8,128)(2,1)} async-done(((bf16[1,256,1024]{2,1,0:T(8,128)(2,1)}), bf16[1,256,4096]{2,1,0:T(8,128)(2,1)}) %all-gather.6.cloned.1.call-update) | async-done | bytes 2097168 | tf_op jit(solution)/shard_map/all_gather | solution.py:33
  47.8 2.1 fusion
  49.8 2.2 fusion.1
  52.0 3.7 gather_fusion
  56.3 1.2 bitcast_select_fusion
  57.5 73.9 %all-gather.12.cloned.1.call-done = bf16[4096,1024]{1,0:T(8,128)(2,1)} async-done(((bf16[512,1024]{1,0:T(8,128)(2,1)}), bf16[4096,1024]{1,0:T(8,128)(2,1)}) %all-gather.12.cloned.1.call-update) | async-done | bytes 8388624 | tf_op jit(solution)/shard_map/all_gather | solution.py:44
  131.4 4.7 %convolution_bitcast_fusion.2 = f32[16,8,8,128]{3,1,2,0:T(8,128)S(1)} fusion(bf16[4096,1024]{1,0:T(8,128)(2,1)} %all-gather.12.cloned.1.call-done, bf16[128,4096]{1,0:T(8,128)(2,1)S(1)} %gather_fusion, pred[128]{0:T(512)(128)(4,1)S(1)} %compare_and_fusion), kind=kOutput, calls=%fused_computation.11 | convolution fusion | flops 1074266112 | bytes 9961600 | tf_op jit(solution)/shard_map/dot_general | solution.py:48
  136.5 77.1 %all-gather.10.cloned.1.call-done = bf16[4096,1024]{1,0:T(8,128)(2,1)} async-done(((bf16[512,1024]{1,0:T(8,128)(2,1)}), bf16[4096,1024]{1,0:T(8,128)(2,1)}) %all-gather.10.cloned.1.call-update) | async-done | bytes 8388624 | tf_op jit(solution)/shard_map/all_gather | solution.py:45
  213.6 12.1 %copy.27 = bf16[1024,4096]{1,0:T(8,128)(2,1)} copy(bf16[1024,4096]{0,1:T(8,128)(2,1)} %bitcast.131) | data formatting | bytes 16777216 | tf_op jit(solution)/shard_map/dot_general | solution.py:49
  225.7 69.9 %all-gather.8.cloned.1.call-done = bf16[4096,1024]{1,0:T(8,128)(2,1)} async-done(((bf16[512,1024]{1,0:T(8,128)(2,1)}), bf16[4096,1024]{1,0:T(8,128)(2,1)}) %all-gather.8.cloned.1.call-update) | async-done | bytes 8388624 | tf_op jit(solution)/shard_map/all_gather | solution.py:43
  295.6 5.9 %fusion.7 = f32[32,8,8,128]{3,1,2,0:T(8,128)S(1)} fusion(bf16[4096,1024]{1,0:T(8,128)(2,1)} %all-gather.8.cloned.1.call-done, bf16[1,256,4096]{2,1,0:T(8,128)(2,1)S(1)} %fusion.1), kind=kOutput, calls=%fused_computation.8 | convolution fusion | flops 2147745792 | bytes 11534336 | tf_op jit(solution)/shard_map/dot_general | solution.py:47
  301.7 1.2 fusion.12
  303.2 2.9 convolution_bitcast_fusion.3
  306.1 1.1 fusion.17
  307.2 1.0 fusion.10
  308.3 1.2 fusion.13
  309.9 67.7 %all-gather.14.cloned.1.call-done = bf16[1024,4096]{1,0:T(8,128)(2,1)} async-done(((bf16[1024,512]{1,0:T(8,128)(2,1)}), bf16[1024,4096]{1,0:T(8,128)(2,1)}) %all-gather.14.cloned.1.call-update) | async-done | bytes 8388624 | tf_op jit(solution)/shard_map/all_gather | solution.py:60
  377.6 7.7 %fusion.25 = f32[256,4096]{1,0:T(8,128)} fusion(bf16[1024,4096]{1,0:T(8,128)(2,1)} %all-gather.14.cloned.1.call-done, bf16[32,8,8,128]{3,2,1,0:T(8,128)(2,1)S(1)} %bitcast.136), kind=kOutput, calls=%fused_computation.36 | convolution fusion | flops 2147483648 | bytes 13107200 | tf_op jit(solution)/shard_map/dot_general | solution.py:58
  385.4 1.1 fusion.19
  386.5 1.8 fusion.11
  388.3 48.3 %reduce-scatter.2.cloned.1.call-done = f32[256,1024]{1,0:T(8,128)} async-done(((f32[256,4096]{1,0:T(8,128)}), f32[256,1024]{1,0:T(8,128)}) %reduce-scatter.2.cloned.1.call-update) | async-done | bytes 1048592 | tf_op jit(solution)/shard_map/reduce_scatter | solution.py:63
  436.6 2.2 fusion.24
  (40 shorter events, 5.4 us)
Async XLA Ops:
  7.2 40.6 %all-gather.6.cloned.1.call-start = ((), (), s32[]{:S(2)}) async-start(), calls=%async_computation.1 | async-start | bytes 2621440 | tf_op jit(solution)/shard_map/all_gather | solution.py:33
  7.9 123.5 %all-gather.12.cloned.1.call-start = ((), (), s32[]{:S(2)}) async-start(), calls=%async_computation.4 | async-start | bytes 9437184 | tf_op jit(solution)/shard_map/all_gather | solution.py:44
  8.6 204.9 %all-gather.10.cloned.1.call-start = ((), (), s32[]{:S(2)}) async-start(), calls=%async_computation.3 | async-start | bytes 9437184 | tf_op jit(solution)/shard_map/all_gather | solution.py:45
  9.4 286.2 %all-gather.8.cloned.1.call-start = ((), (), s32[]{:S(2)}) async-start(), calls=%async_computation.2 | async-start | bytes 9437184 | tf_op jit(solution)/shard_map/all_gather | solution.py:43
  10.0 367.6 %all-gather.14.cloned.1.call-start = ((), (), s32[]{:S(2)}) async-start(), calls=%async_computation.5 | async-start | bytes 9437184 | tf_op jit(solution)/shard_map/all_gather | solution.py:60
  10.5 426.0 %reduce-scatter.2.cloned.1.call-start = ((), (), s32[]{:S(2)}) async-start(), calls=%async_computation.6 | async-start | bytes 5242880 | tf_op jit(solution)/shard_map/reduce_scatter | solution.py:63
  225.7 76.1 %copy-start.1 = (f32[1,8,128,128]{3,2,1,0:T(8,128)S(1)}, f32[1,8,128,128]{3,2,1,0:T(8,128)}, u32[]{:S(2)}) copy-start(f32[1,8,128,128]{3,2,1,0:T(8,128)} %param.15) | copy-start | bytes 1572868
  295.6 7.6 %copy-start = (bf16[1024,4096]{1,0:T(8,128)(2,1)S(1)}, bf16[1024,4096]{1,0:T(8,128)(2,1)}, u32[]{:S(2)}) copy-start(bf16[1024,4096]{1,0:T(8,128)(2,1)} %copy.27) | copy-start | bytes 25165828
  295.6 7.6 %copy-start.2 = (bf16[1,128,1,1,1,1,4096]{6,1,5,4,3,2,0:T(8,128)(2,1)S(1)}, bf16[1,128,1,1,1,1,4096]{6,1,5,4,3,2,0:T(8,128)(2,1)}, u32[]{:S(2)}) copy-start(bf16[1,128,1,1,1,1,4096]{6,1,5,4,3,2,0:T(8,128)(2,1)} %bitcast_select_fusion) | copy-start | bytes 3145732
  377.6 59.0 %copy-start.3 = (bf16[1,256,1024]{2,1,0:T(8,128)(2,1)S(1)}, bf16[1,256,1024]{2,1,0:T(8,128)(2,1)}, u32[]{:S(2)}) copy-start(bf16[1,256,1024]{2,1,0:T(8,128)(2,1)} %param.8) | copy-start | bytes 1572868
Sparse Core Ops, SparseCore 0:
  9.8 37.8 all-gather.5
  49.3 82.0 all-gather.11
  133.0 80.5 all-gather.9
  215.0 80.5 all-gather.7
  297.0 80.5 all-gather.13
  385.5 51.0 reduce-scatter.1
where the time goes:
time: 446 us
  waiting for transfers between devices  360 us (81%)
  matrix products  29.1 us (7%)
  local copies, waits for them, and re-layouts  16.9 us (4%)
  blocking collectives  15.9 us (4%)
  between operations  14.3 us (3%)
  other arithmetic  8.83 us (2%)
    all_gather x1, waiting for transfers between devices, body(): piece_value = lax.all_gather(w_value, 'batch', axis=0, tiled=True)  77.1 us
    all_gather x1, waiting for transfers between devices, body(): piece_key = lax.all_gather(w_key, 'batch', axis=0, tiled=True)  73.9 us
    all_gather x1, waiting for transfers between devices, body(): piece_query = lax.all_gather(w_query, 'batch', axis=0, tiled=True)  69.9 us
    all_gather x1, waiting for transfers between devices, body(): lax.all_gather(w_out, 'batch', axis=1, tiled=True)  67.7 us
    reduce_scatter x1, waiting for transfers between devices, body(): mixed = lax.psum_scatter(terms, 'head', scatter_dimension=1, tiled=True)  48.3 us
    all_gather x1, waiting for transfers between devices, body(): whole = lax.all_gather(hidden_in, 'head', axis=2, tiled=True)  20.3 us
    all_gather x1, blocking collectives, body(): piece_beta = lax.all_gather(w_beta, 'batch', axis=0, tiled=True)  15.9 us
    dot_general x1, local copies, waits for them, and re-layouts, body(): jnp.dot(memory_rows, piece_value, preferred_element_type=jnp.float32)  12.1 us
  transfers between devices with their start and end apart: 6, of which 6 were waited for; matrix products, arithmetic and copies ran while one was open for 10% of the time, Pallas kernels for 0%

commit v1 on v0

--- a/solution.py
+++ b/solution.py
@@ -40,7 +40,9 @@
     memory_rows = jax.vmap(lambda block, where: jnp.take(block, where, axis=0))(normed, picked)
     memory_rows = memory_rows.reshape(seq_count * SEGS * mem_count, full_width)
     token_rows = normed.reshape(seq_count * row_count, full_width)
-    piece_query = lax.all_gather(w_query, "batch", axis=0, tiled=True)
+    piece_query = jnp.concatenate(
+        lax.all_to_all(jnp.stack([w_query] * lax.axis_size("batch")), "batch", 0, 0), axis=0
+    )
     piece_key = lax.all_gather(w_key, "batch", axis=0, tiled=True)
     piece_value = lax.all_gather(w_value, "batch", axis=0, tiled=True)
     piece_beta = lax.all_gather(w_beta, "batch", axis=0, tiled=True)

time: 446 us -> 494 us (1.11)
  blocking collectives: 15.9 us -> 320 us
  waiting for transfers between devices: 360 us -> 93 us
  starting transfers between devices: 0.23 us -> 6.67 us
    all_gather x1, blocking collectives: 15.9 us -> 320 us  [body(): piece_beta = lax.all_gather(w_beta, 'batch', axis=0, tiled=True)]
    all_gather x1, waiting for transfers between devices: 77.1 us -> 0.01 us  [body(): piece_value = lax.all_gather(w_value, 'batch', axis=0, tiled=True)]
    all_gather x1, waiting for transfers between devices: 73.9 us -> 0.01 us  [body(): piece_key = lax.all_gather(w_key, 'batch', axis=0, tiled=True)]
    all_gather x1 -> x0, waiting for transfers between devices: 69.9 us -> none  [body(): piece_query = lax.all_gather(w_query, 'batch', axis=0, tiled=True)]
    all_gather x1, waiting for transfers between devices: 67.7 us -> 42.1 us  [body(): lax.all_gather(w_out, 'batch', axis=1, tiled=True)]
    all_gather x1, waiting for transfers between devices: 20.3 us -> 0.02 us  [body(): whole = lax.all_gather(hidden_in, 'head', axis=2, tiled=True)]
    all_to_all x0 -> x1, starting transfers between devices: none -> 6.49 us  [body(): lax.all_to_all(jnp.stack([w_query] * lax.axis_size('batch')), 'batch', 0, 0)]
    another operation x0 -> x1, local copies, waits for them, and re-layouts: none -> 5.54 us  [body(): jnp.stack([w_query] * lax.axis_size('batch'))]
  transfers between devices with their start and end apart: 6 -> 6, of which waited for: 6 -> 2; matrix products, arithmetic and copies ran while one was open for 10% -> 10% of each run, Pallas kernels for 0% -> 0%
where the time goes in v1:
time: 494 us; the launch traced here: 493 us
  blocking collectives  320 us (65%)
  waiting for transfers between devices  93 us (19%)
  matrix products  29.9 us (6%)
  local copies, waits for them, and re-layouts  21.6 us (4%)
  between operations  14 us (3%)
  other arithmetic  8.13 us (2%)
  starting transfers between devices  6.67 us (1%)
    all_gather x1, blocking collectives, body(): piece_beta = lax.all_gather(w_beta, 'batch', axis=0, tiled=True)  320 us
    reduce_scatter x1, waiting for transfers between devices, body(): mixed = lax.psum_scatter(terms, 'head', scatter_dimension=1, tiled=True)  48.3 us
    all_gather x1, waiting for transfers between devices, body(): lax.all_gather(w_out, 'batch', axis=1, tiled=True)  42.1 us
    dot_general x1, local copies, waits for them, and re-layouts, body(): jnp.dot(memory_rows, piece_value, preferred_element_type=jnp.float32)  11.2 us
  transfers between devices with their start and end apart: 6, of which 2 were waited for; matrix products, arithmetic and copies ran while one was open for 10% of the time, Pallas kernels for 0%

profile of v1, /device:TPU:0, one launch (start us, length us, event | category | flops | bytes accessed | tf_op | source)
XLA Modules:
  0.0 493.0 jit_solution(12469135170158348019)
XLA Ops:
  7.2 0.7 all-gather.5.cloned.1.call-update
  7.9 0.7 all-gather.9.cloned.1.call-update
  8.7 0.7 all-gather.7.cloned.1.call-update
  9.4 5.5 %stack.8 = bf16[8,512,1024]{2,1,0:T(8,128)(2,1)} broadcast(bf16[512,1024]{1,0:T(8,128)(2,1)} %param.9), dimensions={1,2} | broadcast | bytes 9437184 | tf_op jit(solution)/shard_map/stack | solution.py:44
  14.9 6.5 %all-to-all-start = ((bf16[8,512,1024]{2,1,0:T(8,128)(2,1)}), bf16[8,512,1024]{2,1,0:T(8,128)(2,1)}, u32[]{:S(2)}, u32[]{:S(2)}) async-start(bf16[8,512,1024]{2,1,0:T(8,128)(2,1)} %stack.8), calls=%async_computation | async-start | bytes 16777216 | tf_op jit(solution)/shard_map/all_to_all | solution.py:44
  22.3 319.7 %all_gather.16 = bf16[4096,8]{0,1:T(8,128)(2,1)S(1)} all-gather(bf16[512,8]{0,1:T(8,128)(2,1)S(1)} %copy-done.4), channel_id=1, replica_groups=mesh['head'=4,'batch'=8] {'batch'}, dimensions={0}, use_global_device_ids=true | all-gather | bytes 73728 | tf_op jit(solution)/shard_map/all_gather | solution.py:48
  342.1 2.1 fusion
  344.2 2.2 fusion.1
  346.4 3.7 gather_fusion
  350.7 1.1 bitcast_select_fusion
  351.8 5.3 %convolution_bitcast_fusion.2 = f32[16,8,8,128]{3,1,2,0:T(8,128)S(1)} fusion(bf16[4096,1024]{1,0:T(8,128)(2,1)} %all-gather.9.cloned.1.call-done, bf16[128,4096]{1,0:T(8,128)(2,1)S(1)} %gather_fusion, pred[128]{0:T(512)(128)(4,1)S(1)} %compare_and_fusion), kind=kOutput, calls=%fused_computation.11 | convolution fusion | flops 1074266112 | bytes 9961600 | tf_op jit(solution)/shard_map/dot_general | solution.py:50
  357.5 11.2 %copy.27 = bf16[1024,4096]{1,0:T(8,128)(2,1)} copy(bf16[1024,4096]{0,1:T(8,128)(2,1)} %bitcast.132) | data formatting | bytes 16777216 | tf_op jit(solution)/shard_map/dot_general | solution.py:51
  368.8 6.0 %fusion.7 = f32[32,8,8,128]{3,1,2,0:T(8,128)S(1)} fusion(bf16[4096,1024]{1,0:T(8,128)(2,1)} %bitcast.1, bf16[1,256,4096]{2,1,0:T(8,128)(2,1)S(1)} %fusion.1), kind=kOutput, calls=%fused_computation.8 | convolution fusion | flops 2147745792 | bytes 11534336 | tf_op jit(solution)/shard_map/dot_general | solution.py:49
  375.0 1.3 fusion.12
  376.5 2.9 convolution_bitcast_fusion.3
  379.4 1.1 fusion.17
  380.6 1.0 fusion.10
  381.6 1.3 fusion.13
  383.2 42.1 %all-gather.11.cloned.1.call-done = bf16[1024,4096]{1,0:T(8,128)(2,1)} async-done(((bf16[1024,512]{1,0:T(8,128)(2,1)}), bf16[1024,4096]{1,0:T(8,128)(2,1)}) %all-gather.11.cloned.1.call-update) | async-done | bytes 8388624 | tf_op jit(solution)/shard_map/all_gather | solution.py:62
  425.3 7.7 %fusion.25 = f32[256,4096]{1,0:T(8,128)} fusion(bf16[1024,4096]{1,0:T(8,128)(2,1)} %all-gather.11.cloned.1.call-done, bf16[32,8,8,128]{3,2,1,0:T(8,128)(2,1)S(1)} %bitcast.137), kind=kOutput, calls=%fused_computation.36 | convolution fusion | flops 2147483648 | bytes 13107200 | tf_op jit(solution)/shard_map/dot_general | solution.py:60
  433.1 1.1 fusion.19
  434.2 1.8 fusion.11
  436.0 48.3 %reduce-scatter.2.cloned.1.call-done = f32[256,1024]{1,0:T(8,128)} async-done(((f32[256,4096]{1,0:T(8,128)}), f32[256,1024]{1,0:T(8,128)}) %reduce-scatter.2.cloned.1.call-update) | async-done | bytes 1048592 | tf_op jit(solution)/shard_map/reduce_scatter | solution.py:65
  484.3 2.2 fusion.24
  (44 shorter events, 2.9 us)
Async XLA Ops:
  7.2 334.9 %all-gather.5.cloned.1.call-start = ((), (), s32[]{:S(2)}) async-start(), calls=%async_computation.2 | async-start | bytes 2621440 | tf_op jit(solution)/shard_map/all_gather | solution.py:33
  7.9 343.9 %all-gather.9.cloned.1.call-start = ((), (), s32[]{:S(2)}) async-start(), calls=%async_computation.4 | async-start | bytes 9437184 | tf_op jit(solution)/shard_map/all_gather | solution.py:46
  8.6 348.9 %all-gather.7.cloned.1.call-start = ((), (), s32[]{:S(2)}) async-start(), calls=%async_computation.3 | async-start | bytes 9437184 | tf_op jit(solution)/shard_map/all_gather | solution.py:47
  14.9 7.1 %copy-start.5 = (s32[1,2,64]{2,1,0:T(2,128)S(1)}, s32[1,2,64]{2,1,0:T(2,128)}, u32[]{:S(2)}) copy-start(s32[1,2,64]{2,1,0:T(2,128)} %param.14) | copy-start | bytes 1540
  14.9 7.4 %copy-start.4 = (bf16[512,8]{0,1:T(8,128)(2,1)S(1)}, bf16[512,8]{0,1:T(8,128)(2,1)}, u32[]{:S(2)}) copy-start(bf16[512,8]{0,1:T(8,128)(2,1)} %param.12) | copy-start | bytes 24580
  14.9 353.8 %all-to-all-start = ((bf16[8,512,1024]{2,1,0:T(8,128)(2,1)}), bf16[8,512,1024]{2,1,0:T(8,128)(2,1)}, u32[]{:S(2)}, u32[]{:S(2)}) async-start(bf16[8,512,1024]{2,1,0:T(8,128)(2,1)} %stack.8), calls=%async_computation | async-start | bytes 16777216 | tf_op jit(solution)/shard_map/all_to_all | solution.py:44
  21.4 403.9 %all-gather.11.cloned.1.call-start = ((), (), s32[]{:S(2)}) async-start(), calls=%async_computation.5 | async-start | bytes 9437184 | tf_op jit(solution)/shard_map/all_gather | solution.py:62
  22.0 462.3 %reduce-scatter.2.cloned.1.call-start = ((), (), s32[]{:S(2)}) async-start(), calls=%async_computation.6 | async-start | bytes 5242880 | tf_op jit(solution)/shard_map/reduce_scatter | solution.py:65
  368.8 6.3 %copy-start.1 = (f32[1,8,128,128]{3,2,1,0:T(8,128)S(1)}, f32[1,8,128,128]{3,2,1,0:T(8,128)}, u32[]{:S(2)}) copy-start(f32[1,8,128,128]{3,2,1,0:T(8,128)} %param.15) | copy-start | bytes 1572868
  368.8 7.8 %copy-start = (bf16[1024,4096]{1,0:T(8,128)(2,1)S(1)}, bf16[1024,4096]{1,0:T(8,128)(2,1)}, u32[]{:S(2)}) copy-start(bf16[1024,4096]{1,0:T(8,128)(2,1)} %copy.27) | copy-start | bytes 25165828
  368.8 7.8 %copy-start.2 = (bf16[1,128,1,1,1,1,4096]{6,1,5,4,3,2,0:T(8,128)(2,1)S(1)}, bf16[1,128,1,1,1,1,4096]{6,1,5,4,3,2,0:T(8,128)(2,1)}, u32[]{:S(2)}) copy-start(bf16[1,128,1,1,1,1,4096]{6,1,5,4,3,2,0:T(8,128)(2,1)} %bitcast_select_fusion) | copy-start | bytes 3145732
  425.3 59.0 %copy-start.3 = (bf16[1,256,1024]{2,1,0:T(8,128)(2,1)S(1)}, bf16[1,256,1024]{2,1,0:T(8,128)(2,1)}, u32[]{:S(2)}) copy-start(bf16[1,256,1024]{2,1,0:T(8,128)(2,1)} %param.8) | copy-start | bytes 1572868
Sparse Core Ops, SparseCore 0:
  9.8 37.8 all-gather.4
  49.4 187.8 all-gather.8
  238.8 103.8 all-gather.6
  344.2 81.0 all-gather.10
  433.2 51.0 reduce-scatter.1
